TPU v7x, 512 devices: a whole 4x8x8 slice. The times are simulated.
512 devices in a mesh: dp: 2 (over core), tensor: 4 (over x), expert: 64 (over y, z).
Axes of the slice: x: 4, y: 8, z: 8, core: 2. Of those that a mesh axis runs over, the one named last changes fastest.
Arguments:
- checkpoint: bfloat16 [16384, 2048], P(('dp', 'expert'), 'tensor'), may hold values from -6 to 6
- scales: float32 [16384], P(('dp', 'expert')), may hold values from 0.5 to 2
- out_grad: bfloat16 [16384, 2048], P(('dp', 'expert'), 'tensor'), may hold values from -1.5 to 1.5
- expert_ids: int32 [16384, 8], P(('dp', 'expert')), may hold values from 0 to 127, all different within a row; in each aligned block of 128 rows (0 to 127, 128 to 255, ...) at most 8 rows name the same one
- gates: float32 [16384, 8], P(('dp', 'expert')), may hold values from 0.05 to 1
- w_gate: bfloat16 [128, 768, 2048], P(('dp', 'expert'), 'tensor'), may hold values from -0.125 to 0.125
- w_up: bfloat16 [128, 768, 2048], P(('dp', 'expert'), 'tensor'), may hold values from -0.125 to 0.125
- w_down: bfloat16 [128, 768, 2048], P(('dp', 'expert'), 'tensor'), may hold values from -0.21875 to 0.21875
Outputs:
- grad_input: bfloat16 [16384, 2048], P(('dp', 'expert'), 'tensor')
- grad_gates: float32 [16384, 8], P(('dp', 'expert'))
Inputs may be any that keep to these rules, and one draw needn't show every extreme that they name: `expert_ids`: each row names 8 different experts. Among the 128 rows of one device (aligned blocks of rows), no expert is named more than 8 times, a bound that some block reaches.
All inputs are finite; a program needn't handle non-finite values.
Results may differ from a plain program's by a relative error of at most 0.012.
Values may be sent and summed in bfloat16 or wider, within the bound.
A program may use at most 64 MiB of HBM per device.

v0:
```python
import jax
import jax.numpy as jnp
from jax import lax
from jax.sharding import PartitionSpec as P


def body(checkpoint, scales, out_grad, expert_ids, gates, w_gate, w_up, w_down):
    f32, bf16 = (jnp.float32, jnp.bfloat16)
    planes = lax.axis_size("tensor")
    experts = lax.axis_size("dp") * lax.axis_size("expert")
    rank = lax.axis_index("tensor")
    tokens, part = checkpoint.shape
    picks = expert_ids.shape[1]
    cap = tokens * picks // experts
    own = cap // planes
    width = part * planes
    wg = lax.all_gather(w_gate[0], "tensor", axis=0, tiled=True)
    wu = lax.all_gather(w_up[0], "tensor", axis=0, tiled=True)
    wd = lax.all_gather(w_down[0], "tensor", axis=0, tiled=True)
    dequant = (checkpoint.astype(f32) * scales[:, None]).astype(bf16)
    both = lax.all_gather(jnp.stack([dequant, out_grad]), "tensor", axis=2, tiled=True)
    named = expert_ids[:, :, None] == jnp.arange(experts, dtype=jnp.int32)[None, None, :]
    member = jnp.any(named, axis=1)
    weight = jnp.sum(jnp.where(named, gates[:, :, None], 0.0), axis=1)
    lower = (jnp.arange(tokens)[:, None] > jnp.arange(tokens)[None, :]).astype(bf16)
    place = jnp.dot(lower, member.astype(bf16), preferred_element_type=f32).astype(jnp.int32)
    slots = rank * own + jnp.arange(own, dtype=jnp.int32)
    pick = member.T[:, None, :] & (place.T[:, None, :] == slots[None, :, None])
    pick_rows = pick.reshape(experts * own, tokens)
    one = pick_rows.astype(bf16)
    send_x = jnp.dot(one, both[0], preferred_element_type=f32).astype(bf16)
    send_g = jnp.dot(one, both[1], preferred_element_type=f32).astype(bf16)
    names = ("dp", "expert")
    rows = lax.all_to_all(send_x.reshape(experts, own, width), names, 0, 0, tiled=True)
    grads = lax.all_to_all(send_g.reshape(experts, own, width), names, 0, 0, tiled=True)
    rows = rows.reshape(experts * own, width)
    grads = grads.reshape(experts * own, width)
    contract = (((1,), (1,)), ((), ()))
    gate_pre = lax.dot_general(rows, wg, contract, preferred_element_type=f32)
    up_pre = lax.dot_general(rows, wu, contract, preferred_element_type=f32)
    back = lax.dot_general(grads, wd, contract, preferred_element_type=f32)
    sigma = jax.nn.sigmoid(gate_pre)
    swish = gate_pre * sigma
    hidden = (swish * up_pre).astype(bf16)
    gate_term = jnp.sum(hidden.astype(f32) * back, axis=1)
    d_gate = (back * up_pre * sigma * (1.0 + gate_pre * (1.0 - sigma))).astype(bf16)
    d_up = (back * swish).astype(bf16)
    result = jnp.dot(d_gate, wg, preferred_element_type=f32)
    result = result + jnp.dot(d_up, wu, preferred_element_type=f32)
    tail = jnp.broadcast_to(gate_term[:, None], (experts * own, 128))
    packed = jnp.concatenate([result.astype(bf16), tail.astype(bf16)], axis=1)
    came = lax.all_to_all(packed.reshape(experts, own, width + 128), names, 0, 0, tiled=True)
    came = came.reshape(experts * own, width + 128)
    combine = jnp.where(pick, weight.T[:, None, :], 0.0).reshape(experts * own, tokens)
    high = combine.astype(bf16)
    low = (combine - high.astype(f32)).astype(bf16)
    flip = (((0,), (0,)), ((), ()))
    mixed = lax.dot_general(high, came[:, :width], flip, preferred_element_type=f32)
    mixed = mixed + lax.dot_general(low, came[:, :width], flip, preferred_element_type=f32)
    term = jnp.sum(
        jnp.where(pick, came[:, width].astype(f32).reshape(experts, own)[:, :, None], 0.0), axis=1
    )
    terms = jnp.sum(jnp.where(named, term.T[:, None, :], 0.0), axis=2)
    terms = jnp.pad(terms, ((0, 0), (0, 128 - picks))).astype(bf16)
    joined = jnp.concatenate(
        [
            mixed.astype(bf16).reshape(tokens, planes, part),
            jnp.broadcast_to(terms[:, None], (tokens, planes, 128)),
        ],
        axis=2,
    ).transpose(1, 0, 2)
    summed = lax.psum_scatter(joined, "tensor", scatter_dimension=0, tiled=True)[0]
    return (summed[:, :part], summed[:, part : part + picks].astype(f32))


def solution(mesh):
    return jax.shard_map(
        body,
        mesh=mesh,
        in_specs=(
            P(("dp", "expert"), "tensor"),
            P(("dp", "expert")),
            P(("dp", "expert"), "tensor"),
            P(("dp", "expert"), None),
            P(("dp", "expert"), None),
            P(("dp", "expert"), "tensor", None),
            P(("dp", "expert"), "tensor", None),
            P(("dp", "expert"), "tensor", None),
        ),
        out_specs=(P(("dp", "expert"), "tensor"), P(("dp", "expert"), None)),
        check_vma=False,
    )
```

profile of v0, /device:TPU:8, one launch (start us, length us, event | category | flops | bytes accessed | tf_op | source)
XLA Modules:
  0.0 274.9 jit_solution(13853421694187391772)
XLA Ops:
  7.2 1.0 fusion.24
  8.2 1.6 pad_maximum_fusion.1
  9.9 0.7 all-gather.14.cloned.1.call-update
  10.7 0.7 all-gather.12.cloned.1.call-update
  12.3 31.8 %all-gather.8.cloned.1.call-done = bf16[2,128,2048]{2,1,0:T(8,128)(2,1)} async-done(((bf16[2,128,512]{2,1,0:T(8,128)(2,1)}), bf16[2,128,2048]{2,1,0:T(8,128)(2,1)}) %all-gather.8.cloned.1.call-update) | async-done | bytes 1048592 | tf_op jit(solution)/shard_map/all_gather | solution.py:21
  44.1 1.5 convolution_convert_fusion
  45.6 1.5 reshape.113
  47.1 14.2 %all-to-all-start.1 = ((bf16[128,2,2048]{2,1,0:T(2,128)(2,1)}), bf16[128,2,2048]{2,1,0:T(2,128)(2,1)S(1)}, u32[]{:S(2)}, u32[]{:S(2)}) async-start(bf16[128,2,2048]{2,1,0:T(2,128)(2,1)} %reshape.113), calls=%async_computation.1 | async-start | bytes 2097152 | tf_op jit(solution)/shard_map/all_to_all | solution.py:34
  61.3 0.5 all-gather.10.cloned.1.call-update
  62.3 1.5 reshape.111
  63.8 28.5 %all-to-all-done.1 = bf16[128,2,2048]{2,1,0:T(2,128)(2,1)S(1)} async-done(((bf16[128,2,2048]{2,1,0:T(2,128)(2,1)}), bf16[128,2,2048]{2,1,0:T(2,128)(2,1)S(1)}, u32[]{:S(2)}, u32[]{:S(2)}) %all-to-all-start.1) | async-done | bytes 1048608 | tf_op jit(solution)/shard_map/all_to_all | solution.py:34
  92.2 7.5 %all-to-all-start = ((bf16[128,2,2048]{2,1,0:T(2,128)(2,1)}), bf16[128,2,2048]{2,1,0:T(2,128)(2,1)S(1)}, u32[]{:S(2)}, u32[]{:S(2)}) async-start(bf16[128,2,2048]{2,1,0:T(2,128)(2,1)} %reshape.111), calls=%async_computation | async-start | bytes 2097152 | tf_op jit(solution)/shard_map/all_to_all | solution.py:35
  99.7 0.4 reshape.114
  100.2 30.6 %all-to-all-done = bf16[128,2,2048]{2,1,0:T(2,128)(2,1)S(1)} async-done(((bf16[128,2,2048]{2,1,0:T(2,128)(2,1)}), bf16[128,2,2048]{2,1,0:T(2,128)(2,1)S(1)}, u32[]{:S(2)}, u32[]{:S(2)}) %all-to-all-start) | async-done | bytes 1048608 | tf_op jit(solution)/shard_map/all_to_all | solution.py:35
  131.2 3.0 %fusion.2 = f32[256,768]{1,0:T(8,128)S(1)} fusion(bf16[256,2048]{1,0:T(8,128)(2,1)S(1)} %reshape.114, bf16[1,768,2048]{2,1,0:T(8,128)(2,1)} %all-gather.14.cloned.1.call-done), kind=kOutput, calls=%fused_computation.2 | convolution fusion | flops 805306368 | bytes 4980736 | tf_op jit(solution)/shard_map/dot_general | solution.py:39
  134.3 4.4 %all-gather.12.cloned.1.call-done = bf16[1,768,2048]{2,1,0:T(8,128)(2,1)} async-done(((bf16[1,192,2048]{2,1,0:T(8,128)(2,1)}), bf16[1,768,2048]{2,1,0:T(8,128)(2,1)}) %all-gather.12.cloned.1.call-update) | async-done | bytes 3145744 | tf_op jit(solution)/shard_map/all_gather | solution.py:18
  138.6 3.9 %fusion.6 = f32[256,768]{1,0:T(8,128)} fusion(bf16[256,2048]{1,0:T(8,128)(2,1)S(1)} %reshape.114, bf16[1,768,2048]{2,1,0:T(8,128)(2,1)} %all-gather.12.cloned.1.call-done), kind=kOutput, calls=%fused_computation.6 | convolution fusion | flops 805306368 | bytes 4980736 | tf_op jit(solution)/shard_map/dot_general | solution.py:40
  142.5 43.1 %all-gather.10.cloned.1.call-done = bf16[1,768,2048]{2,1,0:T(8,128)(2,1)} async-done(((bf16[1,192,2048]{2,1,0:T(8,128)(2,1)}), bf16[1,768,2048]{2,1,0:T(8,128)(2,1)}) %all-gather.10.cloned.1.call-update) | async-done | bytes 3145744 | tf_op jit(solution)/shard_map/all_gather | solution.py:19
  185.7 3.4 %multiply_reduce_fusion = (bf16[256]{0:T(256)(128)(2,1)S(1)}, f32[256,768]{1,0:T(8,128)S(1)}) fusion(f32[256,768]{1,0:T(8,128)} %fusion.6, f32[256,768]{1,0:T(8,128)S(1)} %fusion.2, bf16[256,2048]{1,0:T(8,128)(2,1)S(1)} %reshape.112, bf16[1,768,2048]{2,1,0:T(8,128)(2,1)} %all-gather.10.cloned.1.call-done), kind=kOutput, calls=%fused_computation.21 | convolution fusion | flops 807075584 | bytes 6554112 | tf_op jit(solution)/shard_map/dot_general | solution.py:41
  189.1 1.2 fusion
  190.3 0.7 copy-done.4
  191.0 1.1 fusion.13
  192.3 1.3 reshape.115
  193.5 14.3 %all-to-all-start.2 = ((bf16[128,2,2176]{2,1,0:T(2,128)(2,1)}), bf16[128,2,2176]{2,1,0:T(2,128)(2,1)S(1)}, u32[]{:S(2)}, u32[]{:S(2)}) async-start(bf16[128,2,2176]{2,1,0:T(2,128)(2,1)} %reshape.115), calls=%async_computation.2 | async-start | bytes 2228224 | tf_op jit(solution)/shard_map/all_to_all | solution.py:52
  208.4 32.1 %all-to-all-done.2 = bf16[128,2,2176]{2,1,0:T(2,128)(2,1)S(1)} async-done(((bf16[128,2,2176]{2,1,0:T(2,128)(2,1)}), bf16[128,2,2176]{2,1,0:T(2,128)(2,1)S(1)}, u32[]{:S(2)}, u32[]{:S(2)}) %all-to-all-start.2) | async-done | bytes 1114144 | tf_op jit(solution)/shard_map/all_to_all | solution.py:52
  240.4 0.4 reshape.116
  241.6 0.5 select_reduce_fusion.1
  243.6 0.9 maximum_bitcast_fusion
  244.5 21.0 %reduce-scatter.2.cloned.1.call-done = bf16[1,128,640]{1,2,0:T(8,128)(2,1)} async-done(((bf16[4,128,640]{1,2,0:T(8,128)(2,1)}), bf16[1,128,640]{1,2,0:T(8,128)(2,1)}) %reduce-scatter.2.cloned.1.call-update) | async-done | bytes 163856 | tf_op jit(solution)/shard_map/reduce_scatter | solution.py:72
  265.5 0.9 slice.29
  266.4 1.3 slice_convert_fusion
  267.6 0.8 copy.36
  (48 shorter events, 4.7 us)
Async XLA Ops:
  7.2 4.2 %copy-start.1 = (s32[128,8]{0,1:T(8,128)S(1)}, s32[128,8]{0,1:T(8,128)}, u32[]{:S(2)}) copy-start(s32[128,8]{0,1:T(8,128)} %param.11) | copy-start | bytes 12292
  7.2 36.9 %all-gather.8.cloned.1.call-start = ((), (), s32[]{:S(2)}) async-start(), calls=%async_computation.4 | async-start | bytes 1310720 | tf_op jit(solution)/shard_map/all_gather | solution.py:21
  9.9 121.3 %all-gather.14.cloned.1.call-start = ((), (), s32[]{:S(2)}) async-start(), calls=%async_computation.8 | async-start | bytes 3932160 | tf_op jit(solution)/shard_map/all_gather | solution.py:17
  10.6 128.0 %all-gather.12.cloned.1.call-start = ((), (), s32[]{:S(2)}) async-start(), calls=%async_computation.7 | async-start | bytes 3932160 | tf_op jit(solution)/shard_map/all_gather | solution.py:18
  45.6 16.2 %copy-start = (bf16[2,128,2048]{2,1,0:T(8,128)(2,1)S(1)}, bf16[2,128,2048]{2,1,0:T(8,128)(2,1)}, u32[]{:S(2)}) copy-start(bf16[2,128,2048]{2,1,0:T(8,128)(2,1)} %all-gather.8.cloned.1.call-done) | copy-start | bytes 3145732
  47.1 45.2 %all-to-all-start.1 = ((bf16[128,2,2048]{2,1,0:T(2,128)(2,1)}), bf16[128,2,2048]{2,1,0:T(2,128)(2,1)S(1)}, u32[]{:S(2)}, u32[]{:S(2)}) async-start(bf16[128,2,2048]{2,1,0:T(2,128)(2,1)} %reshape.113), calls=%async_computation.1 | async-start | bytes 2097152 | tf_op jit(solution)/shard_map/all_to_all | solution.py:34
  61.2 124.4 %all-gather.10.cloned.1.call-start = ((), (), s32[]{:S(2)}) async-start(), calls=%async_computation.6 | async-start | bytes 3932160 | tf_op jit(solution)/shard_map/all_gather | solution.py:19
  92.2 38.5 %all-to-all-start = ((bf16[128,2,2048]{2,1,0:T(2,128)(2,1)}), bf16[128,2,2048]{2,1,0:T(2,128)(2,1)S(1)}, u32[]{:S(2)}, u32[]{:S(2)}) async-start(bf16[128,2,2048]{2,1,0:T(2,128)(2,1)} %reshape.111), calls=%async_computation | async-start | bytes 2097152 | tf_op jit(solution)/shard_map/all_to_all | solution.py:35
  185.7 3.4 %copy-start.3 = (bf16[1,768,2048]{2,1,0:T(8,128)(2,1)S(1)}, bf16[1,768,2048]{2,1,0:T(8,128)(2,1)}, u32[]{:S(2)}) copy-start(bf16[1,768,2048]{2,1,0:T(8,128)(2,1)} %all-gather.14.cloned.1.call-done) | copy-start | bytes 9437188
  185.7 3.4 %copy-start.5 = (f32[256,768]{1,0:T(8,128)S(1)}, f32[256,768]{1,0:T(8,128)}, u32[]{:S(2)}) copy-start(f32[256,768]{1,0:T(8,128)} %fusion.6) | copy-start | bytes 2359300
  189.1 1.9 copy-start.4
  192.3 15.7 %copy-start.2 = (f32[128,8]{0,1:T(8,128)S(1)}, f32[128,8]{0,1:T(8,128)}, u32[]{:S(2)}) copy-start(f32[128,8]{0,1:T(8,128)} %param.12) | copy-start | bytes 12292
  193.5 46.9 %all-to-all-start.2 = ((bf16[128,2,2176]{2,1,0:T(2,128)(2,1)}), bf16[128,2,2176]{2,1,0:T(2,128)(2,1)S(1)}, u32[]{:S(2)}, u32[]{:S(2)}) async-start(bf16[128,2,2176]{2,1,0:T(2,128)(2,1)} %reshape.115), calls=%async_computation.2 | async-start | bytes 2228224 | tf_op jit(solution)/shard_map/all_to_all | solution.py:52
  207.9 57.6 %reduce-scatter.2.cloned.1.call-start = ((), (), s32[]{:S(2)}) async-start(), calls=%async_computation.5 | async-start | bytes 819200 | tf_op jit(solution)/shard_map/reduce_scatter | solution.py:72
Sparse Core Ops, SparseCore 0:
  10.1 33.9 all-gather.7
  46.2 45.2 all-gather.13
  93.6 45.0 all-gather.11
  140.6 45.0 all-gather.9
  244.6 20.8 reduce-scatter.1
where the time goes:
time: 276 us; the launch traced here: 275 us
  waiting for transfers between devices  193 us (70%)
  starting transfers between devices  36.2 us (13%)
  matrix products  15.5 us (6%)
  between operations  14.1 us (5%)
  local copies, waits for them, and re-layouts  9.56 us (3%)
  other arithmetic  6.24 us (2%)
    all_gather x1, waiting for transfers between devices, body(): wd = lax.all_gather(w_down[0], 'tensor', axis=0, tiled=True)  43.1 us
    all_to_all x1, waiting for transfers between devices, body(): lax.all_to_all(packed.reshape(experts, own, width + 128), names, 0, 0, ti...  32.1 us
    all_gather x1, waiting for transfers between devices, body(): lax.all_gather(jnp.stack([dequant, out_grad]), 'tensor', axis=2, tiled=True)  31.8 us
    all_to_all x1, waiting for transfers between devices, body(): lax.all_to_all(send_g.reshape(experts, own, width), names, 0, 0, tiled=True)  30.6 us
    all_to_all x1, waiting for transfers between devices, body(): lax.all_to_all(send_x.reshape(experts, own, width), names, 0, 0, tiled=True)  28.5 us
    reduce_scatter x1, waiting for transfers between devices, body(): lax.psum_scatter(joined, 'tensor', scatter_dimension=0, tiled=True)[0]  21 us
    all_to_all x1, starting transfers between devices, body(): lax.all_to_all(packed.reshape(experts, own, width + 128), names, 0, 0, ti...  14.3 us
    all_to_all x1, starting transfers between devices, body(): lax.all_to_all(send_x.reshape(experts, own, width), names, 0, 0, tiled=True)  14.2 us
  transfers between devices with their start and end apart: 8, of which 7 were waited for; matrix products, arithmetic and copies ran while one was open for 5% of the time, Pallas kernels for 0%

commit v1 on v0

--- a/solution.py
+++ b/solution.py
@@ -2,6 +2,11 @@
 import jax.numpy as jnp
 from jax import lax
 from jax.sharding import PartitionSpec as P
+
+target_hold = lambda mine, which_dim: jnp.concatenate(
+    lax.all_to_all(jnp.stack([mine for _ in range(lax.axis_size("tensor"))]), "tensor", 0, 0),
+    axis=which_dim,
+)
 
 
 def body(checkpoint, scales, out_grad, expert_ids, gates, w_gate, w_up, w_down):
@@ -16,7 +21,7 @@
     width = part * planes
     wg = lax.all_gather(w_gate[0], "tensor", axis=0, tiled=True)
     wu = lax.all_gather(w_up[0], "tensor", axis=0, tiled=True)
-    wd = lax.all_gather(w_down[0], "tensor", axis=0, tiled=True)
+    wd = target_hold(w_down[0], 0)
     dequant = (checkpoint.astype(f32) * scales[:, None]).astype(bf16)
     both = lax.all_gather(jnp.stack([dequant, out_grad]), "tensor", axis=2, tiled=True)
     named = expert_ids[:, :, None] == jnp.arange(experts, dtype=jnp.int32)[None, None, :]

time: 276 us -> 263 us (0.953)
  waiting for transfers between devices: 193 us -> 145 us
  blocking collectives: 0 us -> 38.4 us
  starting transfers between devices: 36.2 us -> 30.2 us
    all_gather x1 -> x0, waiting for transfers between devices: 43.1 us -> none  [body(): wd = lax.all_gather(w_down[0], 'tensor', axis=0, tiled=True)]
    all_to_all x0 -> x1, blocking collectives: none -> 38.4 us  [body(): lax.all_to_all(send_g.reshape(experts, own, width), names, 0, 0, tiled=True)]
    all_gather x1, waiting for transfers between devices: 4.39 us -> 0.02 us  [body(): wu = lax.all_gather(w_up[0], 'tensor', axis=0, tiled=True)]
    all_to_all x1, starting transfers between devices: 14.3 us -> 11.1 us  [body(): lax.all_to_all(packed.reshape(experts, own, width + 128), names, 0, 0, ti...]
  transfers between devices with their start and end apart: 8 -> 7, of which waited for: 7 -> 5; matrix products, arithmetic and copies ran while one was open for 5% -> 6% of each run, Pallas kernels for 0% -> 0%
where the time goes in v1:
time: 263 us; the launch traced here: 262 us
  waiting for transfers between devices  145 us (55%)
  blocking collectives  38.4 us (15%)
  starting transfers between devices  30.2 us (11%)
  matrix products  16.6 us (6%)
  between operations  14.1 us (5%)
  local copies, waits for them, and re-layouts  11.6 us (4%)
  other arithmetic  6.23 us (2%)
    all_to_all x1, blocking collectives, body(): lax.all_to_all(send_g.reshape(experts, own, width), names, 0, 0, tiled=True)  38.4 us
    all_to_all x1, waiting for transfers between devices, body(): lax.all_to_all(packed.reshape(experts, own, width + 128), names, 0, 0, ti...  32.1 us
    all_gather x1, waiting for transfers between devices, body(): lax.all_gather(jnp.stack([dequant, out_grad]), 'tensor', axis=2, tiled=True)  31.8 us
    all_to_all x1, waiting for transfers between devices, lax.all_to_all(jnp.stack([mine for _ in range(lax.axis_size('tensor'))]),...  29.9 us
    all_to_all x1, waiting for transfers between devices, body(): lax.all_to_all(send_x.reshape(experts, own, width), names, 0, 0, tiled=True)  29.1 us
    reduce_scatter x1, waiting for transfers between devices, body(): lax.psum_scatter(joined, 'tensor', scatter_dimension=0, tiled=True)[0]  20.7 us
    all_to_all x1, starting transfers between devices, body(): lax.all_to_all(send_x.reshape(experts, own, width), names, 0, 0, tiled=True)  14.2 us
    all_to_all x1, starting transfers between devices, body(): lax.all_to_all(packed.reshape(experts, own, width + 128), names, 0, 0, ti...  11.1 us
  transfers between devices with their start and end apart: 7, of which 5 were waited for; matrix products, arithmetic and copies ran while one was open for 6% of the time, Pallas kernels for 0%

profile of v1, /device:TPU:8, one launch (start us, length us, event | category | flops | bytes accessed | tf_op | source)
XLA Modules:
  0.0 262.2 jit_solution(8399379794772489551)
XLA Ops:
  7.2 1.0 fusion.22
  8.2 1.6 pad_maximum_fusion.1
  9.9 0.7 all-gather.10.cloned.1.call-update
  10.6 0.8 copy.29
  12.3 31.8 %all-gather.6.cloned.1.call-done = bf16[2,128,2048]{2,1,0:T(8,128)(2,1)} async-done(((bf16[2,128,512]{2,1,0:T(8,128)(2,1)}), bf16[2,128,2048]{2,1,0:T(8,128)(2,1)}) %all-gather.6.cloned.1.call-update) | async-done | bytes 1048592 | tf_op jit(solution)/shard_map/all_gather | solution.py:26
  44.1 1.5 convolution_convert_fusion
  45.6 1.5 reshape.118
  47.1 14.2 %all-to-all-start.2 = ((bf16[128,2,2048]{2,1,0:T(2,128)(2,1)}), bf16[128,2,2048]{2,1,0:T(2,128)(2,1)S(1)}, u32[]{:S(2)}, u32[]{:S(2)}) async-start(bf16[128,2,2048]{2,1,0:T(2,128)(2,1)} %reshape.118), calls=%async_computation.2 | async-start | bytes 2097152 | tf_op jit(solution)/shard_map/all_to_all | solution.py:39
  61.3 0.7 all-gather.8.cloned.1.call-update
  62.5 0.7 reshape.115
  63.2 29.1 %all-to-all-done.2 = bf16[128,2,2048]{2,1,0:T(2,128)(2,1)S(1)} async-done(((bf16[128,2,2048]{2,1,0:T(2,128)(2,1)}), bf16[128,2,2048]{2,1,0:T(2,128)(2,1)S(1)}, u32[]{:S(2)}, u32[]{:S(2)}) %all-to-all-start.2) | async-done | bytes 1048608 | tf_op jit(solution)/shard_map/all_to_all | solution.py:39
  92.3 38.4 %all_to_all.20 = bf16[128,2,2048]{2,1,0:T(2,128)(2,1)S(1)} all-to-all(bf16[128,2,2048]{2,1,0:T(2,128)(2,1)S(1)} %reshape.115), channel_id=1, replica_groups=mesh['dp'=2,'tensor'=4,'expert'=64] {'dp','expert'}, dimensions={0} | all-to-all | bytes 2097152 | tf_op jit(solution)/shard_map/all_to_all | solution.py:40
  130.7 2.0 stack.15
  132.8 4.8 %all-to-all-start.1 = ((bf16[4,192,2048]{2,1,0:T(8,128)(2,1)}), bf16[4,192,2048]{2,1,0:T(8,128)(2,1)}, u32[]{:S(2)}, u32[]{:S(2)}) async-start(bf16[4,192,2048]{2,1,0:T(8,128)(2,1)} %stack.15), calls=%async_computation.1 | async-start | bytes 6291456 | tf_op jit(solution)/shard_map/all_to_all | solution.py:7
  137.6 0.4 reshape.119
  138.5 2.9 %fusion.2 = f32[256,768]{1,0:T(8,128)S(1)} fusion(bf16[256,2048]{1,0:T(8,128)(2,1)S(1)} %reshape.119, bf16[1,768,2048]{2,1,0:T(8,128)(2,1)} %all-gather.10.cloned.1.call-done), kind=kOutput, calls=%fused_computation.2 | convolution fusion | flops 805306368 | bytes 4980736 | tf_op jit(solution)/shard_map/dot_general | solution.py:44
  141.5 4.1 %fusion.6 = f32[256,768]{1,0:T(8,128)} fusion(bf16[256,2048]{1,0:T(8,128)(2,1)S(1)} %reshape.119, bf16[1,768,2048]{2,1,0:T(8,128)(2,1)} %all-gather.8.cloned.1.call-done), kind=kOutput, calls=%fused_computation.6 | convolution fusion | flops 805306368 | bytes 4980736 | tf_op jit(solution)/shard_map/dot_general | solution.py:45
  145.5 29.9 %all-to-all-done.1 = bf16[4,192,2048]{2,1,0:T(8,128)(2,1)} async-done(((bf16[4,192,2048]{2,1,0:T(8,128)(2,1)}), bf16[4,192,2048]{2,1,0:T(8,128)(2,1)}, u32[]{:S(2)}, u32[]{:S(2)}) %all-to-all-start.1) | async-done | bytes 3145760 | tf_op jit(solution)/shard_map/all_to_all | solution.py:7
  175.5 3.4 %multiply_reduce_fusion = (bf16[256]{0:T(256)(128)(2,1)S(1)}, f32[256,768]{1,0:T(8,128)S(1)}) fusion(f32[256,768]{1,0:T(8,128)} %fusion.6, f32[256,768]{1,0:T(8,128)S(1)} %fusion.2, bf16[256,2048]{1,0:T(8,128)(2,1)S(1)} %reshape.116, bf16[768,2048]{1,0:T(8,128)(2,1)} %bitcast.8), kind=kOutput, calls=%fused_computation.19 | convolution fusion | flops 807075584 | bytes 6554112 | tf_op jit(solution)/shard_map/dot_general | solution.py:46
  178.9 1.1 fusion
  180.0 0.7 copy-done.4
  180.8 2.2 fusion.11
  183.2 1.3 reshape.120
  184.4 11.1 %all-to-all-start.3 = ((bf16[128,2,2176]{2,1,0:T(2,128)(2,1)}), bf16[128,2,2176]{2,1,0:T(2,128)(2,1)S(1)}, u32[]{:S(2)}, u32[]{:S(2)}) async-start(bf16[128,2,2176]{2,1,0:T(2,128)(2,1)} %reshape.120), calls=%async_computation.3 | async-start | bytes 2228224 | tf_op jit(solution)/shard_map/all_to_all | solution.py:57
  196.0 32.1 %all-to-all-done.3 = bf16[128,2,2176]{2,1,0:T(2,128)(2,1)S(1)} async-done(((bf16[128,2,2176]{2,1,0:T(2,128)(2,1)}), bf16[128,2,2176]{2,1,0:T(2,128)(2,1)S(1)}, u32[]{:S(2)}, u32[]{:S(2)}) %all-to-all-start.3) | async-done | bytes 1114144 | tf_op jit(solution)/shard_map/all_to_all | solution.py:57
  228.1 0.4 reshape.121
  229.2 0.5 select_reduce_fusion.1
  231.2 0.9 maximum_bitcast_fusion
  232.1 20.7 %reduce-scatter.2.cloned.1.call-done = bf16[1,128,640]{1,2,0:T(8,128)(2,1)} async-done(((bf16[4,128,640]{1,2,0:T(8,128)(2,1)}), bf16[1,128,640]{1,2,0:T(8,128)(2,1)}) %reduce-scatter.2.cloned.1.call-update) | async-done | bytes 163856 | tf_op jit(solution)/shard_map/reduce_scatter | solution.py:77
  252.8 0.9 slice.29
  253.7 1.3 slice_convert_fusion
  254.9 0.8 copy.36
  (49 shorter events, 4.6 us)
Async XLA Ops:
  7.2 36.9 %all-gather.6.cloned.1.call-start = ((), (), s32[]{:S(2)}) async-start(), calls=%async_computation.5 | async-start | bytes 1310720 | tf_op jit(solution)/shard_map/all_gather | solution.py:26
  9.9 128.6 %all-gather.10.cloned.1.call-start = ((), (), s32[]{:S(2)}) async-start(), calls=%async_computation.8 | async-start | bytes 3932160 | tf_op jit(solution)/shard_map/all_gather | solution.py:22
  45.6 16.5 %copy-start = (bf16[2,128,2048]{2,1,0:T(8,128)(2,1)S(1)}, bf16[2,128,2048]{2,1,0:T(8,128)(2,1)}, u32[]{:S(2)}) copy-start(bf16[2,128,2048]{2,1,0:T(8,128)(2,1)} %all-gather.6.cloned.1.call-done) | copy-start | bytes 3145732
  47.1 45.2 %all-to-all-start.2 = ((bf16[128,2,2048]{2,1,0:T(2,128)(2,1)}), bf16[128,2,2048]{2,1,0:T(2,128)(2,1)S(1)}, u32[]{:S(2)}, u32[]{:S(2)}) async-start(bf16[128,2,2048]{2,1,0:T(2,128)(2,1)} %reshape.118), calls=%async_computation.2 | async-start | bytes 2097152 | tf_op jit(solution)/shard_map/all_to_all | solution.py:39
  61.3 80.2 %all-gather.8.cloned.1.call-start = ((), (), s32[]{:S(2)}) async-start(), calls=%async_computation.7 | async-start | bytes 3932160 | tf_op jit(solution)/shard_map/all_gather | solution.py:23
  92.3 38.4 %copy-start.1 = (bf16[1,192,2048]{2,1,0:T(8,128)(2,1)S(1)}, bf16[1,192,2048]{2,1,0:T(8,128)(2,1)}, u32[]{:S(2)}) copy-start(bf16[1,192,2048]{2,1,0:T(8,128)(2,1)} %param.15) | copy-start | bytes 2359300
  132.8 42.7 %all-to-all-start.1 = ((bf16[4,192,2048]{2,1,0:T(8,128)(2,1)}), bf16[4,192,2048]{2,1,0:T(8,128)(2,1)}, u32[]{:S(2)}, u32[]{:S(2)}) async-start(bf16[4,192,2048]{2,1,0:T(8,128)(2,1)} %stack.15), calls=%async_computation.1 | async-start | bytes 6291456 | tf_op jit(solution)/shard_map/all_to_all | solution.py:7
  141.4 37.4 %copy-start.5 = (f32[256,768]{1,0:T(8,128)}, f32[256,768]{1,0:T(8,128)S(1)}, u32[]{:S(2)}) copy-start(f32[256,768]{1,0:T(8,128)S(1)} %fusion.2) | copy-start | bytes 2359300
  175.5 3.4 %copy-start.3 = (bf16[1,768,2048]{2,1,0:T(8,128)(2,1)S(1)}, bf16[1,768,2048]{2,1,0:T(8,128)(2,1)}, u32[]{:S(2)}) copy-start(bf16[1,768,2048]{2,1,0:T(8,128)(2,1)} %all-gather.10.cloned.1.call-done) | copy-start | bytes 9437188
  175.5 3.4 %copy-start.6 = (f32[256,768]{1,0:T(8,128)S(1)}, f32[256,768]{1,0:T(8,128)}, u32[]{:S(2)}) copy-start(f32[256,768]{1,0:T(8,128)} %fusion.6) | copy-start | bytes 2359300
  178.9 1.9 copy-start.4
  183.2 12.4 %copy-start.2 = (f32[128,8]{0,1:T(8,128)S(1)}, f32[128,8]{0,1:T(8,128)}, u32[]{:S(2)}) copy-start(f32[128,8]{0,1:T(8,128)} %param.12) | copy-start | bytes 12292
  184.4 43.6 %all-to-all-start.3 = ((bf16[128,2,2176]{2,1,0:T(2,128)(2,1)}), bf16[128,2,2176]{2,1,0:T(2,128)(2,1)S(1)}, u32[]{:S(2)}, u32[]{:S(2)}) async-start(bf16[128,2,2176]{2,1,0:T(2,128)(2,1)} %reshape.120), calls=%async_computation.3 | async-start | bytes 2228224 | tf_op jit(solution)/shard_map/all_to_all | solution.py:57
  195.5 57.3 %reduce-scatter.2.cloned.1.call-start = ((), (), s32[]{:S(2)}) async-start(), calls=%async_computation.6 | async-start | bytes 819200 | tf_op jit(solution)/shard_map/reduce_scatter | solution.py:77
Sparse Core Ops, SparseCore 0:
  10.1 33.9 all-gather.5
  46.2 45.2 all-gather.9
  93.5 45.0 all-gather.7
  232.2 20.5 reduce-scatter.1
